TPU v7x, 32 devices: a whole 2x2x4 slice. The times are simulated.
32 devices in a mesh: grp: 2 (over y), skill: 16 (over z, x, core).
Axes of the slice: x: 2, y: 2, z: 4, core: 2. Of those that a mesh axis runs over, the one named last changes fastest.
Arguments:
- value_next: bfloat16 [2048, 4, 2048], P('skill', 'grp'), parts along dimension 1, may hold values from -6 to 6
- income_matrix: float32 [64, 32], P('grp'), parts along dimension 0, may hold values from -1 to 1
- block_weights: bfloat16 [16, 16, 4, 128, 128], P('skill')
- block_offset: int32 [16, 16, 4], P('skill'), may hold values from 0 to 3, as said below
- block_count: int32 [16, 16], P('skill'), may hold values from 1 to 4, as said below
- asset_next: int32 [16, 2, 2048], replicated, may hold values from 0 to 1
- flow: float32 [32, 2, 2048], P('grp'), parts along dimension 0, may hold values from -4 to 15
Outputs:
- value_now: bfloat16 [2048, 4, 2048], P('skill', 'grp'), parts along dimension 1
There are 2 independent parts, one for each index of `grp`. A program takes and returns all parts, laid end to end along the dimension named above; an argument that names none is the same for every part. Nothing has to cross between parts.
Inputs may be any that keep to these rules, and one draw needn't show every extreme that they name: `block_offset`: each row of 4 entries is a permutation of 0 to 3, the same for every level. `block_count`: the same for every level.
All inputs are finite; a program needn't handle non-finite values.
Results may differ from a plain program's by a relative error of at most 0.0031.
Values may be sent and summed in bfloat16 or wider, within the bound.
A program may use at most 128 MiB of HBM per device.

v0:
```python
import functools
import math

import jax
import jax.numpy as jnp
from jax import lax
from jax.experimental import pallas as pl
from jax.experimental.pallas import tpu as pltpu
from jax.sharding import PartitionSpec as P

def shifted(block, axis, distance):
    devices = range(lax.axis_size(axis))
    route = [(i - distance, i) for i in devices if i - distance in devices]
    return lax.ppermute(block, axis, route)


def on_device_split(
    value_next, income_matrix, block_weights, block_offset, block_count, asset_next, flow
):
    tiles = lax.axis_size("skill")
    local_rows, assets, skills = value_next.shape
    tile = skills // tiles
    rows = local_rows * tiles
    shocks = income_matrix.shape[0]
    parents = rows // shocks
    blocks = block_offset.shape[-1]
    levels = block_offset.shape[1]
    arrived = lax.all_to_all(value_next, "skill", split_axis=2, concat_axis=0, tiled=True)
    width = arrived.shape[2]
    grid = arrived.astype(jnp.float32).reshape(parents, shocks, assets * width)
    mixed = jnp.einsum("fe,hex->hfx", income_matrix, grid, precision=lax.Precision.HIGHEST)
    own_tile = mixed.reshape(rows, assets, width).astype(jnp.bfloat16)
    gathered = [own_tile]
    for step in range(1, blocks):
        gathered.append(shifted(own_tile, "skill", -step))
    window = jnp.concatenate(gathered, axis=2)
    matrix = window.reshape(rows * assets, blocks * tile)
    place = jnp.arange(blocks, dtype=jnp.int32)
    offsets = block_offset[0]
    counts = block_count[0]
    select = (
        (offsets[:, :, None] == place[None, None, :])
        & (place[None, :, None] < counts[:, None, None])
    ).astype(jnp.float32)
    transit = jnp.einsum("ikr,ikst->irts", select, block_weights[0].astype(jnp.float32))
    transit = transit.astype(jnp.bfloat16).reshape(levels, blocks * tile, tile)
    flow_rows = jnp.transpose(flow, (0, 2, 1))[..., None]
    choose = jnp.transpose(asset_next, (0, 2, 1))

    def level_step(index, carry):
        running_max, running_total = carry
        cont = jnp.dot(matrix, transit[index], preferred_element_type=jnp.float32).reshape(
            rows, assets, tile
        )
        chosen = choose[index][:, :, None]
        picked = jnp.zeros((rows, assets, tile), jnp.float32)
        for option in range(assets):
            picked = picked + jnp.where(chosen == option, cont[:, option : option + 1, :], 0.0)
        score = (flow_rows[index] + 0.96 * picked) / 0.05
        new_max = jnp.maximum(running_max, score)
        new_total = running_total * jnp.exp(running_max - new_max) + jnp.exp(score - new_max)
        return (new_max, new_total)

    start_max = jnp.full((rows, assets, tile), -jnp.inf, jnp.float32)
    start_total = jnp.zeros((rows, assets, tile), jnp.float32)
    final_max, final_total = lax.fori_loop(0, levels, level_step, (start_max, start_total))
    value_tile = (0.05 * (final_max + jnp.log(final_total))).astype(jnp.bfloat16)
    return lax.all_to_all(value_tile, "skill", split_axis=0, concat_axis=2, tiled=True)


SUB = 16
STEP = 32
SCALE = math.log2(math.e) / 0.05


def split_three(mix):
    high = mix.astype(jnp.bfloat16)
    rest = mix - high.astype(jnp.float32)
    middle = rest.astype(jnp.bfloat16)
    low = (rest - middle.astype(jnp.float32)).astype(jnp.bfloat16)
    return high, middle, low


def arrange_weights(t, tiles, weights, offsets, counts, sorted_weights):
    levels, blocks, tile, _ = weights.shape

    def one_level(i, carry):
        for r in range(blocks):
            total = jnp.zeros((tile, tile), jnp.float32)
            for k in range(blocks):
                live = (offsets[k] == r) & (counts > k) & (t + r < tiles)
                total = total + jnp.where(live, weights[i, k].astype(jnp.float32), 0.0)
            total = total.astype(jnp.bfloat16)
            for q in range(tile // STEP):
                sorted_weights[q, pl.ds(pl.multiple_of(i * STEP, STEP), STEP), r * tile : (r + 1) * tile] = total[
                    q * STEP : (q + 1) * STEP
                ]
        return carry

    lax.fori_loop(0, levels, one_level, 0)


def one_chunk(window, flow, choose, sorted_weights, scaled, chosen, cont, value, levels, rows):
    for a in range(2):
        scaled[a] = flow[:, a, :] * SCALE
        chosen[a] = choose[:, a, :]
    steps = sorted_weights.shape[0]

    def multiply(q):
        cont[q % 2] = lax.dot_general(
            sorted_weights[q], window, (((1,), (1,)), ((), ())), preferred_element_type=jnp.float32
        )

    def reduce(q):
        for part in range(STEP // SUB):
            for a in range(2):
                scores = []
                for i in range(levels):
                    at = i * STEP + part * SUB
                    first = cont[q % 2, at : at + SUB, :rows]
                    second = cont[q % 2, at : at + SUB, rows:]
                    picked = jnp.where(chosen[a, i : i + 1, :] == 1, second, first)
                    scores.append(scaled[a, i : i + 1, :] + (0.96 * SCALE) * picked)
                top = scores
                while len(top) > 1:
                    top = [jnp.maximum(x, y) for x, y in zip(top[::2], top[1::2])]
                terms = [jnp.exp2(x - top[0]) for x in scores]
                while len(terms) > 1:
                    terms = [x + y for x, y in zip(terms[::2], terms[1::2])]
                start = q * STEP + part * SUB
                value[a, start : start + SUB, :] = (1.0 / SCALE) * (top[0] + jnp.log2(terms[0]))

    multiply(0)
    for q in range(steps):
        if q + 1 < steps:
            multiply(q + 1)
        reduce(q)

MESH = pl.DeviceIdType.MESH


def fused_kernel(
    tiles,
    offsets,
    counts,
    mix,
    values,
    weights,
    flow,
    choose,
    out,
    expected,
    window,
    sorted_weights,
    results,
    scaled,
    chosen,
    cont,
    value,
    in_send,
    in_recv,
    one_send,
    one_recv,
    two_send,
    two_recv,
    out_send,
    out_recv,
    weight_sems,
    local_sem,
):
    chips = tiles // 2
    levels, blocks, tile, _ = weights.shape
    rows = values.shape[1]
    me = lax.axis_index("skill")
    chip = lax.div(me, 2)
    core = lax.rem(me, 2)
    partner = chip * 2 + 1 - core

    def device(at):
        return {"skill": at * 2 + core}

    def source(step):
        return lax.rem(chip + step, chips)

    barrier = pltpu.get_barrier_semaphore()

    def greet(step, carry):
        pl.semaphore_signal(barrier, inc=1, device_id=device(source(step)), device_id_type=MESH)
        return carry

    lax.fori_loop(1, chips, greet, 0)
    pl.semaphore_signal(barrier, inc=1, device_id={"skill": partner}, device_id_type=MESH)

    parts = split_three(mix[...])

    def mixed(target, a):
        block = values[a, :, pl.ds(pl.multiple_of(target * 2 * tile, 2 * tile), 2 * tile)]
        total = jnp.dot(parts[2], block, preferred_element_type=jnp.float32)
        total = total + jnp.dot(parts[1], block, preferred_element_type=jnp.float32)
        total = total + jnp.dot(parts[0], block, preferred_element_type=jnp.float32)
        return total.astype(jnp.bfloat16)

    def in_copy(target, origin):
        return pltpu.make_async_remote_copy(
            src_ref=expected.at[target],
            dst_ref=window.at[origin, pl.ds(0, 2)],
            send_sem=in_send.at[target],
            recv_sem=in_recv.at[origin],
            device_id=device(target),
            device_id_type=MESH,
        )

    def one_copy(at):
        return pltpu.make_async_remote_copy(
            src_ref=window.at[at, pl.ds(0, 2)],
            dst_ref=window.at[at, pl.ds(2, 2)],
            send_sem=one_send.at[at],
            recv_sem=one_recv.at[at],
            device_id=device(lax.rem(chip + chips - 1, chips)),
            device_id_type=MESH,
        )

    def two_copy(at):
        return pltpu.make_async_remote_copy(
            src_ref=window.at[at, 0],
            dst_ref=window.at[at, 4],
            send_sem=two_send.at[at],
            recv_sem=two_recv.at[at],
            device_id=device(lax.rem(chip + chips - 2, chips)),
            device_id_type=MESH,
        )

    def out_copy(target, origin):
        return pltpu.make_async_remote_copy(
            src_ref=results.at[target],
            dst_ref=out.at[pl.ds(origin * 2, 2)],
            send_sem=out_send.at[target],
            recv_sem=out_recv.at[origin],
            device_id=device(target),
            device_id_type=MESH,
        )

    def weight_copy(which):
        return pltpu.make_async_remote_copy(
            src_ref=sorted_weights.at[which],
            dst_ref=sorted_weights.at[which],
            send_sem=weight_sems.at[0],
            recv_sem=weight_sems.at[1],
            device_id={"skill": partner},
            device_id_type=MESH,
        )

    pl.semaphore_wait(barrier, chips)

    def send_in(step, carry):
        target = lax.rem(chip + chips - step, chips)
        for a in range(2):
            total = mixed(target, a)
            expected[target, 0, a] = total[:, :tile]
            expected[target, 1, a] = total[:, tile:]
        in_copy(target, chip).start()
        return carry

    lax.fori_loop(1, chips, send_in, 0)
    for a in range(2):
        total = mixed(chip, a)
        window[chip, 0, a] = total[:, :tile]
        window[chip, 1, a] = total[:, tile:]

    @pl.when(chip + 1 >= chips)
    def _():
        def clear(at, carry):
            for slot in (2, 3):
                window[at, slot] = jnp.zeros(window.shape[2:], jnp.bfloat16)
            return carry

        lax.fori_loop(0, chips, clear, 0)

    @pl.when(chip + 2 >= chips)
    def _():
        def clear(at, carry):
            window[at, 4] = jnp.zeros(window.shape[2:], jnp.bfloat16)
            return carry

        lax.fori_loop(0, chips, clear, 0)

    def relay(at):
        @pl.when(chip >= 1)
        def _():
            one_copy(at).start()

        @pl.when(chip >= 2)
        def _():
            two_copy(at).start()

    relay(chip)
    arrange_weights(
        me, tiles, weights, [offsets[0, k] for k in range(blocks)], counts[0, 0], sorted_weights.at[core]
    )
    weight_copy(core).start()

    def arrive(step):
        at = source(step)
        in_copy(lax.rem(chip + 1, chips), at).wait_recv()
        relay(at)

    arrive(1)
    arrive(2)
    weight_copy(1 - core).wait_recv()

    def compute(step, carry):
        at = source(step + 2)

        @pl.when(step + 3 < chips)
        def _():
            arrive(step + 3)

        @pl.when(chip + 1 < chips)
        def _():
            one_copy(at).wait_recv()

        @pl.when(chip + 2 < chips)
        def _():
            two_copy(at).wait_recv()

        start = pl.multiple_of((at * 2 + core) * rows, rows)
        flow_here = flow[:, :, pl.ds(start, rows)]
        choose_here = choose[:, :, pl.ds(start, rows)]

        def one_tile(t, inner):
            blocks_here = [window[at, t + r].reshape(2 * rows, tile) for r in range(blocks)]
            one_chunk(
                jnp.concatenate(blocks_here, axis=1),
                flow_here,
                choose_here,
                sorted_weights.at[t],
                scaled,
                chosen,
                cont,
                value,
                levels,
                rows,
            )
            for a in range(2):
                results[at, t, a] = value[a].T.astype(jnp.bfloat16)
            return inner

        lax.fori_loop(0, 2, one_tile, 0)

        @pl.when(at != chip)
        def _():
            out_copy(at, chip).start()

        @pl.when(at == chip)
        def _():
            pltpu.make_async_copy(results.at[chip], out.at[pl.ds(chip * 2, 2)], local_sem).start()

        return carry

    lax.fori_loop(0, chips, compute, 0)

    pltpu.make_async_copy(results.at[chip], out.at[pl.ds(chip * 2, 2)], local_sem).wait()
    weight_copy(core).wait_send()

    def finish(step, carry):
        at = source(step)
        in_copy(at, chip).wait_send()
        out_copy(at, chip).wait_send()
        out_copy(at, at).wait_recv()
        return carry

    lax.fori_loop(1, chips, finish, 0)

    def relayed(at, carry):
        @pl.when(chip >= 1)
        def _():
            one_copy(at).wait_send()

        @pl.when(chip >= 2)
        def _():
            two_copy(at).wait_send()

        return carry

    lax.fori_loop(0, chips, relayed, 0)


def on_device(value_next, income_matrix, block_weights, block_offset, block_count, asset_next, flow):
    tiles = lax.axis_size("skill")
    chips = tiles // 2
    rows, assets, skills = value_next.shape
    tile = skills // tiles
    shocks = income_matrix.shape[0]
    levels, blocks = block_weights.shape[1:3]
    mix = jnp.kron(jnp.eye(rows // shocks, dtype=jnp.float32), income_matrix)
    turned = jnp.transpose(value_next, (1, 0, 2))
    smem = pl.BlockSpec(memory_space=pltpu.SMEM)
    vmem = pl.BlockSpec(memory_space=pltpu.VMEM)
    dma = pltpu.SemaphoreType.DMA
    back = pl.pallas_call(
        functools.partial(fused_kernel, tiles),
        out_shape=jax.ShapeDtypeStruct((tiles, assets, rows, tile), jnp.bfloat16),
        in_specs=[smem, smem, vmem, vmem, vmem, vmem, vmem],
        out_specs=pl.BlockSpec(memory_space=pl.ANY),
        scratch_shapes=[
            pltpu.VMEM((chips, 2, assets, rows, tile), jnp.bfloat16),
            pltpu.VMEM((chips, blocks + 1, assets, rows, tile), jnp.bfloat16),
            pltpu.VMEM((2, tile // STEP, levels * STEP, blocks * tile), jnp.bfloat16),
            pltpu.VMEM((chips, 2, assets, rows, tile), jnp.bfloat16),
            pltpu.VMEM((assets, levels, rows), jnp.float32),
            pltpu.VMEM((assets, levels, rows), jnp.int32),
            pltpu.VMEM((2, levels * STEP, assets * rows), jnp.float32),
            pltpu.VMEM((assets, tile, rows), jnp.float32),
            dma((chips,)),
            dma((chips,)),
            dma((chips,)),
            dma((chips,)),
            dma((chips,)),
            dma((chips,)),
            dma((chips,)),
            dma((chips,)),
            dma((2,)),
            dma,
        ],
        compiler_params=pltpu.CompilerParams(
            collective_id=0, has_side_effects=True, vmem_limit_bytes=48 * 1024 * 1024
        ),
    )(block_offset[0], block_count, mix, turned, block_weights[0], flow, asset_next)
    return jnp.transpose(back, (2, 1, 0, 3)).reshape(rows, assets, skills)


def solution(mesh):
    placed = (
        P("skill", "grp", None),
        P("grp", None),
        P("skill", None, None, None, None),
        P("skill", None, None),
        P("skill", None),
        P(),
        P("grp", None, None),
    )

    def body(value_next, income_matrix, *rest):
        whole = value_next.shape[0] % income_matrix.shape[0] == 0 and mesh.shape["skill"] >= 8
        return (on_device if whole else on_device_split)(value_next, income_matrix, *rest)

    return jax.shard_map(
        body, mesh=mesh, in_specs=placed, out_specs=P("skill", "grp", None), check_vma=False
    )
```

profile of v0, /device:TPU:16, one launch (start us, length us, event | category | flops | bytes accessed | tf_op | source)
XLA Modules:
  0.0 94.8 jit_solution(8208031904143437109)
XLA Ops:
  0.0 0.0 copy-start.1
  0.0 0.0 copy-start.3
  0.0 0.0 copy-start
  0.0 0.9 copy.11.offsets
  0.9 0.8 broadcast_multiply_fusion
  1.8 0.2 mul.27.mix
  1.9 0.0 copy-start.2
  1.9 1.6 %copy.15 = bf16[128,2,2048]{2,0,1:T(8,128)(2,1)S(1)} copy(bf16[128,2,2048]{2,1,0:T(2,128)(2,1)} %param.7) | data formatting | bytes 2097152 | tf_op args[0]
  3.6 0.0 copy-done.1
  3.6 0.0 copy-done.3
  3.6 0.0 copy-done
  3.6 0.0 copy-done.2
  3.6 88.5 %shard_map.73 = bf16[16,2,128,128]{3,2,1,0:T(8,128)(2,1)S(1)} custom-call(s32[16,4]{1,0:T(8,128)S(1)} %copy.11.offsets, s32[1,16]{1,0:T(1,128)S(1)} %copy-done.3, f32[128,128]{1,0:T(8,128)S(1)} %mul.27.mix, bf16[2,128,2048]{2,1,0:T(8,128)(2,1)S(1)} %bitcast.8, bf16[16,4,128,128]{3,2,1,0:T(8,128)(2,1)S(1)} %bitcast.9, f32[16,2,2048]{2,1,0:T(2,128)S(1)} %copy-done.1, ...), custom_call_target="tpu_custom_call" | custom-call | tf_op jit(solution)/shard_map/pallas_call | solution.py:400
  92.1 0.7 copy.12
  92.8 2.0 %copy.13 = bf16[128,2,2048]{2,1,0:T(2,128)(2,1)} copy(bf16[128,2,2048]{0,2,1:T(8,128)(2,1)S(1)} %bitcast.10) | data formatting | bytes 2097152 | tf_op jit(solution)/shard_map/reshape | solution.py:429
  (1 shorter events, 0.0 us)
Async XLA Ops:
  0.0 3.6 %copy-start.1 = (f32[16,2,2048]{2,1,0:T(2,128)S(1)}, f32[16,2,2048]{2,1,0:T(2,128)}, u32[]{:S(2)}) copy-start(f32[16,2,2048]{2,1,0:T(2,128)} %flow.1) | copy-start | bytes 786436
  0.0 3.6 %copy-start.3 = (s32[1,16]{1,0:T(1,128)S(1)}, s32[1,16]{1,0:T(1,128)}, u32[]{:S(2)}) copy-start(s32[1,16]{1,0:T(1,128)} %counts.1) | copy-start | bytes 196
  0.0 3.6 %copy-start = (bf16[1,16,4,128,128]{4,3,2,1,0:T(8,128)(2,1)S(1)}, bf16[1,16,4,128,128]{4,3,2,1,0:T(8,128)(2,1)}, u32[]{:S(2)}) copy-start(bf16[1,16,4,128,128]{4,3,2,1,0:T(8,128)(2,1)} %param.9) | copy-start | bytes 6291460
  1.9 1.7 %copy-start.2 = (s32[16,2,2048]{2,1,0:T(2,128)S(1)}, s32[16,2,2048]{2,1,0:T(2,128)}, u32[]{:S(2)}) copy-start(s32[16,2,2048]{2,1,0:T(2,128)} %choose.1) | copy-start | bytes 786436
where the time goes:
time: 95 us; the launch traced here: 94.8 us
  Pallas kernels  88.5 us (93%)
  local copies, waits for them, and re-layouts  5.39 us (6%)
    pallas_call x1, Pallas kernels, on_device(): pl.pallas_call(functools.partial(fused_kernel, tiles), out_shape=jax.Shap...  88.5 us
    reshape x1, local copies, waits for them, and re-layouts, on_device(): return jnp.transpose(back, (2, 1, 0, 3)).reshape(rows, assets, skills)  2.01 us

commit v1 on v0

--- a/solution.py
+++ b/solution.py
@@ -157,35 +157,50 @@
     chosen,
     cont,
     value,
-    in_send,
-    in_recv,
-    one_send,
-    one_recv,
-    two_send,
-    two_recv,
+    base_send,
+    base_recv,
+    extra_send,
+    extra_recv,
+    trade_send,
+    trade_recv,
+    relay_send,
+    third_recv,
     out_send,
     out_recv,
+    near_sems,
     weight_sems,
     local_sem,
 ):
     chips = tiles // 2
+    planes = chips // 2
     levels, blocks, tile, _ = weights.shape
     rows = values.shape[1]
     me = lax.axis_index("skill")
     chip = lax.div(me, 2)
     core = lax.rem(me, 2)
     partner = chip * 2 + 1 - core
+    z = lax.div(chip, 2)
+    x = lax.rem(chip, 2)
+    high = lax.div(z, planes // 2)
+    toward = 1 - 2 * high
+    beside = z * 2 + 1 - x
 
     def device(at):
         return {"skill": at * 2 + core}
 
-    def source(step):
-        return lax.rem(chip + step, chips)
+    def target_at(step):
+        plane = lax.rem(planes // 2 - high + toward * lax.div(step, 2) + planes, planes)
+        return plane, plane * 2 + lax.rem(x + step, 2)
+
+    def source_at(step):
+        plane = lax.rem(z + toward * (1 + lax.div(step, 2)) + planes, planes)
+        return plane, plane * 2 + lax.rem(step, 2)
 
     barrier = pltpu.get_barrier_semaphore()
 
     def greet(step, carry):
-        pl.semaphore_signal(barrier, inc=1, device_id=device(source(step)), device_id_type=MESH)
+        at = lax.rem(chip + step, chips)
+        pl.semaphore_signal(barrier, inc=1, device_id=device(at), device_id_type=MESH)
         return carry
 
     lax.fori_loop(1, chips, greet, 0)
@@ -200,44 +215,90 @@
         total = total + jnp.dot(parts[0], block, preferred_element_type=jnp.float32)
         return total.astype(jnp.bfloat16)
 
-    def in_copy(target, origin):
+    def remote(source, target, send, recv, at):
         return pltpu.make_async_remote_copy(
-            src_ref=expected.at[target],
-            dst_ref=window.at[origin, pl.ds(0, 2)],
-            send_sem=in_send.at[target],
-            recv_sem=in_recv.at[origin],
-            device_id=device(target),
+            src_ref=source,
+            dst_ref=target,
+            send_sem=send,
+            recv_sem=recv,
+            device_id=device(at),
             device_id_type=MESH,
         )
 
-    def one_copy(at):
-        return pltpu.make_async_remote_copy(
-            src_ref=window.at[at, pl.ds(0, 2)],
-            dst_ref=window.at[at, pl.ds(2, 2)],
-            send_sem=one_send.at[at],
-            recv_sem=one_recv.at[at],
-            device_id=device(lax.rem(chip + chips - 1, chips)),
-            device_id_type=MESH,
-        )
-
-    def two_copy(at):
-        return pltpu.make_async_remote_copy(
-            src_ref=window.at[at, 0],
-            dst_ref=window.at[at, 4],
-            send_sem=two_send.at[at],
-            recv_sem=two_recv.at[at],
-            device_id=device(lax.rem(chip + chips - 2, chips)),
-            device_id_type=MESH,
+    def base_copy(target, origin):
+        return remote(
+            expected.at[pl.ds(target * 2, 2)],
+            window.at[origin, pl.ds(0, 2)],
+            base_send.at[target],
+            base_recv.at[origin],
+            target,
+        )
+
+    def left_extra(target, origin):
+        return remote(
+            expected.at[target * 2 + 4],
+            window.at[origin, 4],
+            extra_send.at[target],
+            extra_recv.at[origin],
+            target,
+        )
+
+    def right_extra(target, origin):
+        return remote(
+            expected.at[pl.ds(target * 2 + 3, 2)],
+            window.at[origin, pl.ds(3, 2)],
+            extra_send.at[target],
+            extra_recv.at[origin],
+            target,
+        )
+
+    def near_copy(origin):
+        return remote(
+            expected.at[pl.ds(beside * 2, blocks + 1)],
+            window.at[origin],
+            near_sems.at[0],
+            near_sems.at[1],
+            beside,
+        )
+
+    def trade_right(at):
+        return remote(
+            window.at[at, 4], window.at[at, 2], trade_send.at[at], trade_recv.at[at], beside
+        )
+
+    def trade_left(at):
+        return remote(
+            window.at[at, pl.ds(0, 2)],
+            window.at[at, pl.ds(2, 2)],
+            trade_send.at[at],
+            trade_recv.at[at],
+            beside,
+        )
+
+    below = lax.rem(z + planes - 1, planes) * 2
+
+    def relay_first(at):
+        return remote(
+            window.at[at, 0], window.at[at, 4], relay_send.at[0, at], extra_recv.at[at], below
+        )
+
+    def relay_second(at):
+        return remote(
+            window.at[at, 1], window.at[at, 3], relay_send.at[1, at], extra_recv.at[at], below + 1
+        )
+
+    def relay_third(at):
+        return remote(
+            window.at[at, 0], window.at[at, 4], relay_send.at[0, at], third_recv.at[at], below + 1
         )
 
     def out_copy(target, origin):
-        return pltpu.make_async_remote_copy(
-            src_ref=results.at[target],
-            dst_ref=out.at[pl.ds(origin * 2, 2)],
-            send_sem=out_send.at[target],
-            recv_sem=out_recv.at[origin],
-            device_id=device(target),
-            device_id_type=MESH,
+        return remote(
+            results.at[target],
+            out.at[pl.ds(origin * 2, 2)],
+            out_send.at[target],
+            out_recv.at[origin],
+            target,
         )
 
     def weight_copy(which):
@@ -252,77 +313,115 @@
 
     pl.semaphore_wait(barrier, chips)
 
+    for r in range(blocks - 1):
+        expected[tiles + r] = jnp.zeros(expected.shape[1:], jnp.bfloat16)
+
     def send_in(step, carry):
-        target = lax.rem(chip + chips - step, chips)
+        plane, target = target_at(step)
         for a in range(2):
             total = mixed(target, a)
-            expected[target, 0, a] = total[:, :tile]
-            expected[target, 1, a] = total[:, tile:]
-        in_copy(target, chip).start()
-        return carry
-
-    lax.fori_loop(1, chips, send_in, 0)
-    for a in range(2):
-        total = mixed(chip, a)
-        window[chip, 0, a] = total[:, :tile]
-        window[chip, 1, a] = total[:, tile:]
-
-    @pl.when(chip + 1 >= chips)
+            expected[target * 2, a] = total[:, :tile]
+            expected[target * 2 + 1, a] = total[:, tile:]
+
+        @pl.when(plane != z)
+        def _():
+            base_copy(target, chip).start()
+
+        return carry
+
+    lax.fori_loop(0, chips, send_in, 0)
+    near_copy(chip).start()
+
+    def each_extra(plane, target, act):
+        right = lax.rem(target, 2)
+        wanted = (plane != z) & (plane + 1 < planes) & (z <= plane + 1)
+
+        @pl.when(wanted & (right == 0))
+        def _():
+            act(left_extra(target, chip))
+
+        @pl.when(wanted & (right == 1))
+        def _():
+            act(right_extra(target, chip))
+
+    def send_extra(step, carry):
+        plane, target = target_at(step)
+        each_extra(plane, target, lambda copy: copy.start())
+        return carry
+
+    lax.fori_loop(0, chips, send_extra, 0)
+    for r in range(blocks + 1):
+        window[chip, r] = expected[chip * 2 + r]
+
+    last = z + 1 >= planes
+
+    @pl.when(last)
     def _():
-        def clear(at, carry):
-            for slot in (2, 3):
-                window[at, slot] = jnp.zeros(window.shape[2:], jnp.bfloat16)
+        def clear(step, carry):
+            _, at = source_at(step)
+            window[at, 4] = jnp.zeros(window.shape[2:], jnp.bfloat16)
+
+            @pl.when(x == 1)
+            def _():
+                for slot in (2, 3):
+                    window[at, slot] = jnp.zeros(window.shape[2:], jnp.bfloat16)
+
             return carry
 
-        lax.fori_loop(0, chips, clear, 0)
-
-    @pl.when(chip + 2 >= chips)
-    def _():
-        def clear(at, carry):
-            window[at, 4] = jnp.zeros(window.shape[2:], jnp.bfloat16)
-            return carry
-
-        lax.fori_loop(0, chips, clear, 0)
-
-    def relay(at):
-        @pl.when(chip >= 1)
-        def _():
-            one_copy(at).start()
-
-        @pl.when(chip >= 2)
-        def _():
-            two_copy(at).start()
-
-    relay(chip)
+        lax.fori_loop(0, chips - 2, clear, 0)
+
     arrange_weights(
         me, tiles, weights, [offsets[0, k] for k in range(blocks)], counts[0, 0], sorted_weights.at[core]
     )
     weight_copy(core).start()
 
+    def each_passed(plane, at, act):
+        @pl.when(x == 1)
+        def _():
+            act(trade_left(at))
+
+        passed = (plane > z) & (z >= 1)
+
+        @pl.when(passed & (x == 0))
+        def _():
+            act(relay_first(at))
+            act(relay_second(at))
+
+        @pl.when(passed & (x == 1))
+        def _():
+            act(relay_third(at))
+
     def arrive(step):
-        at = source(step)
-        in_copy(lax.rem(chip + 1, chips), at).wait_recv()
-        relay(at)
-
-    arrive(1)
-    arrive(2)
-    weight_copy(1 - core).wait_recv()
-
-    def compute(step, carry):
-        at = source(step + 2)
-
-        @pl.when(step + 3 < chips)
-        def _():
-            arrive(step + 3)
-
-        @pl.when(chip + 1 < chips)
-        def _():
-            one_copy(at).wait_recv()
-
-        @pl.when(chip + 2 < chips)
-        def _():
-            two_copy(at).wait_recv()
-
+        plane, at = source_at(step)
+        base_copy(chip, at).wait_recv()
+        each_passed(plane, at, lambda copy: copy.start())
+
+        @pl.when((x == 0) & jnp.logical_not(last))
+        def _():
+            left_extra(chip, at).wait_recv()
+            trade_right(at).start()
+
+    def ready(step):
+        plane, at = source_at(step)
+
+        @pl.when(x == 0)
+        def _():
+            trade_left(at).wait_recv()
+
+        @pl.when((x == 1) & jnp.logical_not(last))
+        def _():
+            trade_right(at).wait_recv()
+
+            @pl.when(plane <= z + 1)
+            def _():
+                right_extra(chip, at).wait_recv()
+
+            @pl.when(plane > z + 1)
+            def _():
+                relay_second(at).wait_recv()
+                relay_third(at).wait_recv()
+
+    def compute(at):
         start = pl.multiple_of((at * 2 + core) * rows, rows)
         flow_here = flow[:, :, pl.ds(start, rows)]
         choose_here = choose[:, :, pl.ds(start, rows)]
@@ -347,42 +446,74 @@
 
         lax.fori_loop(0, 2, one_tile, 0)
 
-        @pl.when(at != chip)
+    weight_copy(1 - core).wait_recv()
+
+    def advance(step, carry):
+        distant = lax.max(step - 2, 0)
+        _, far = source_at(distant)
+        same = lax.max(1 - step, 0)
+        next_to = lax.max(1 - lax.max(step - 1, 1 - step), 0)
+        at = same * chip + next_to * beside + (1 - same - next_to) * far
+
+        @pl.when(step == 1)
+        def _():
+            near_copy(beside).wait_recv()
+
+        @pl.when(step >= 2)
+        def _():
+            ready(distant)
+
+        compute(at)
+
+        @pl.when(step >= 1)
         def _():
             out_copy(at, chip).start()
 
-        @pl.when(at == chip)
+        @pl.when(step == 0)
         def _():
             pltpu.make_async_copy(results.at[chip], out.at[pl.ds(chip * 2, 2)], local_sem).start()
 
-        return carry
-
-    lax.fori_loop(0, chips, compute, 0)
+        @pl.when(step + 2 < chips)
+        def _():
+            arrive(step)
+
+        return carry
+
+    lax.fori_loop(0, chips, advance, 0)
 
     pltpu.make_async_copy(results.at[chip], out.at[pl.ds(chip * 2, 2)], local_sem).wait()
     weight_copy(core).wait_send()
+    near_copy(chip).wait_send()
 
     def finish(step, carry):
-        at = source(step)
-        in_copy(at, chip).wait_send()
-        out_copy(at, chip).wait_send()
-        out_copy(at, at).wait_recv()
-        return carry
-
-    lax.fori_loop(1, chips, finish, 0)
-
-    def relayed(at, carry):
-        @pl.when(chip >= 1)
-        def _():
-            one_copy(at).wait_send()
-
-        @pl.when(chip >= 2)
-        def _():
-            two_copy(at).wait_send()
-
-        return carry
-
-    lax.fori_loop(0, chips, relayed, 0)
+        plane, target = target_at(step)
+
+        @pl.when(plane != z)
+        def _():
+            base_copy(target, chip).wait_send()
+
+        each_extra(plane, target, lambda copy: copy.wait_send())
+
+        @pl.when(target != chip)
+        def _():
+            out_copy(target, chip).wait_send()
+            out_copy(target, target).wait_recv()
+
+        return carry
+
+    lax.fori_loop(0, chips, finish, 0)
+
+    def passed_on(step, carry):
+        plane, at = source_at(step)
+        each_passed(plane, at, lambda copy: copy.wait_send())
+
+        @pl.when((x == 0) & jnp.logical_not(last))
+        def _():
+            trade_right(at).wait_send()
+
+        return carry
+
+    lax.fori_loop(0, chips - 2, passed_on, 0)
 
 
 def on_device(value_next, income_matrix, block_weights, block_offset, block_count, asset_next, flow):
@@ -403,7 +534,7 @@
         in_specs=[smem, smem, vmem, vmem, vmem, vmem, vmem],
         out_specs=pl.BlockSpec(memory_space=pl.ANY),
         scratch_shapes=[
-            pltpu.VMEM((chips, 2, assets, rows, tile), jnp.bfloat16),
+            pltpu.VMEM((tiles + blocks - 1, assets, rows, tile), jnp.bfloat16),
             pltpu.VMEM((chips, blocks + 1, assets, rows, tile), jnp.bfloat16),
             pltpu.VMEM((2, tile // STEP, levels * STEP, blocks * tile), jnp.bfloat16),
             pltpu.VMEM((chips, 2, assets, rows, tile), jnp.bfloat16),
@@ -417,8 +548,11 @@
             dma((chips,)),
             dma((chips,)),
             dma((chips,)),
-            dma((chips,)),
-            dma((chips,)),
+            dma((2, chips)),
+            dma((chips,)),
+            dma((chips,)),
+            dma((chips,)),
+            dma((2,)),
             dma((2,)),
             dma,
         ],
@@ -441,7 +575,7 @@
     )
 
     def body(value_next, income_matrix, *rest):
-        whole = value_next.shape[0] % income_matrix.shape[0] == 0 and mesh.shape["skill"] >= 8
+        whole = value_next.shape[0] % income_matrix.shape[0] == 0 and mesh.shape["skill"] % 8 == 0
         return (on_device if whole else on_device_split)(value_next, income_matrix, *rest)
 
     return jax.shard_map(

time: 95 us -> 90.9 us (0.957)
  the two profiles are of different devices: /device:TPU:16 before, /device:TPU:6 now
where the time goes in v1:
time: 90.9 us; the launch traced here: 90.6 us
  Pallas kernels  84.4 us (93%)
  local copies, waits for them, and re-layouts  5.39 us (6%)
    pallas_call x1, Pallas kernels, on_device(): pl.pallas_call(functools.partial(fused_kernel, tiles), out_shape=jax.Shap...  84.4 us
    reshape x1, local copies, waits for them, and re-layouts, on_device(): return jnp.transpose(back, (2, 1, 0, 3)).reshape(rows, assets, skills)  2.01 us

profile of v1, /device:TPU:6, one launch (start us, length us, event | category | flops | bytes accessed | tf_op | source)
XLA Modules:
  0.0 90.6 jit_solution(2218889121046007666)
XLA Ops:
  0.0 0.0 copy-start.1
  0.0 0.0 copy-start.3
  0.0 0.0 copy-start
  0.0 0.9 %copy.11.offsets = s32[16,4]{1,0:T(8,128)S(1)} copy(s32[16,4]{0,1:T(4,128)} %bitcast.11) | data formatting | bytes 512 | tf_op jit(solution)/shard_map/squeeze | solution.py:562
  0.9 0.8 broadcast_multiply_fusion
  1.8 0.2 mul.27.mix
  1.9 0.0 copy-start.2
  1.9 1.6 %copy.15 = bf16[128,2,2048]{2,0,1:T(8,128)(2,1)S(1)} copy(bf16[128,2,2048]{2,1,0:T(2,128)(2,1)} %param.7) | data formatting | bytes 2097152 | tf_op args[0]
  3.6 0.0 copy-done.1
  3.6 0.0 copy-done.3
  3.6 0.0 copy-done
  3.6 0.0 copy-done.2
  3.6 84.4 %shard_map.73 = bf16[16,2,128,128]{3,2,1,0:T(8,128)(2,1)S(1)} custom-call(s32[16,4]{1,0:T(8,128)S(1)} %copy.11.offsets, s32[1,16]{1,0:T(1,128)S(1)} %copy-done.3, f32[128,128]{1,0:T(8,128)S(1)} %mul.27.mix, bf16[2,128,2048]{2,1,0:T(8,128)(2,1)S(1)} %bitcast.8, bf16[16,4,128,128]{3,2,1,0:T(8,128)(2,1)S(1)} %bitcast.9, f32[16,2,2048]{2,1,0:T(2,128)S(1)} %copy-done.1, ...), custom_call_target="tpu_custom_call" | custom-call | tf_op jit(solution)/shard_map/pallas_call | solution.py:531
  88.0 0.7 copy.12
  88.6 2.0 %copy.13 = bf16[128,2,2048]{2,1,0:T(2,128)(2,1)} copy(bf16[128,2,2048]{0,2,1:T(8,128)(2,1)S(1)} %bitcast.10) | data formatting | bytes 2097152 | tf_op jit(solution)/shard_map/reshape | solution.py:563
  (1 shorter events, 0.0 us)
Async XLA Ops:
  0.0 3.6 %copy-start.1 = (f32[16,2,2048]{2,1,0:T(2,128)S(1)}, f32[16,2,2048]{2,1,0:T(2,128)}, u32[]{:S(2)}) copy-start(f32[16,2,2048]{2,1,0:T(2,128)} %flow.1) | copy-start | bytes 786436
  0.0 3.6 %copy-start.3 = (s32[1,16]{1,0:T(1,128)S(1)}, s32[1,16]{1,0:T(1,128)}, u32[]{:S(2)}) copy-start(s32[1,16]{1,0:T(1,128)} %counts.1) | copy-start | bytes 196
  0.0 3.6 %copy-start = (bf16[1,16,4,128,128]{4,3,2,1,0:T(8,128)(2,1)S(1)}, bf16[1,16,4,128,128]{4,3,2,1,0:T(8,128)(2,1)}, u32[]{:S(2)}) copy-start(bf16[1,16,4,128,128]{4,3,2,1,0:T(8,128)(2,1)} %param.9) | copy-start | bytes 6291460
  1.9 1.7 %copy-start.2 = (s32[16,2,2048]{2,1,0:T(2,128)S(1)}, s32[16,2,2048]{2,1,0:T(2,128)}, u32[]{:S(2)}) copy-start(s32[16,2,2048]{2,1,0:T(2,128)} %choose.1) | copy-start | bytes 786436

commit v2 on v0

v2 whole, which is shorter than its diff:
```python
import functools
import math

import jax
import jax.numpy as jnp
from jax import lax
from jax.experimental import pallas as pl
from jax.experimental.pallas import tpu as pltpu
from jax.sharding import PartitionSpec as P

def shifted(block, axis, distance):
    devices = range(lax.axis_size(axis))
    route = [(i - distance, i) for i in devices if i - distance in devices]
    return lax.ppermute(block, axis, route)


def on_device_split(
    value_next, income_matrix, block_weights, block_offset, block_count, asset_next, flow
):
    tiles = lax.axis_size("skill")
    local_rows, assets, skills = value_next.shape
    tile = skills // tiles
    rows = local_rows * tiles
    shocks = income_matrix.shape[0]
    parents = rows // shocks
    blocks = block_offset.shape[-1]
    levels = block_offset.shape[1]
    arrived = lax.all_to_all(value_next, "skill", split_axis=2, concat_axis=0, tiled=True)
    width = arrived.shape[2]
    grid = arrived.astype(jnp.float32).reshape(parents, shocks, assets * width)
    mixed = jnp.einsum("fe,hex->hfx", income_matrix, grid, precision=lax.Precision.HIGHEST)
    own_tile = mixed.reshape(rows, assets, width).astype(jnp.bfloat16)
    gathered = [own_tile]
    for step in range(1, blocks):
        gathered.append(shifted(own_tile, "skill", -step))
    window = jnp.concatenate(gathered, axis=2)
    matrix = window.reshape(rows * assets, blocks * tile)
    place = jnp.arange(blocks, dtype=jnp.int32)
    offsets = block_offset[0]
    counts = block_count[0]
    select = (
        (offsets[:, :, None] == place[None, None, :])
        & (place[None, :, None] < counts[:, None, None])
    ).astype(jnp.float32)
    transit = jnp.einsum("ikr,ikst->irts", select, block_weights[0].astype(jnp.float32))
    transit = transit.astype(jnp.bfloat16).reshape(levels, blocks * tile, tile)
    flow_rows = jnp.transpose(flow, (0, 2, 1))[..., None]
    choose = jnp.transpose(asset_next, (0, 2, 1))

    def level_step(index, carry):
        running_max, running_total = carry
        cont = jnp.dot(matrix, transit[index], preferred_element_type=jnp.float32).reshape(
            rows, assets, tile
        )
        chosen = choose[index][:, :, None]
        picked = jnp.zeros((rows, assets, tile), jnp.float32)
        for option in range(assets):
            picked = picked + jnp.where(chosen == option, cont[:, option : option + 1, :], 0.0)
        score = (flow_rows[index] + 0.96 * picked) / 0.05
        new_max = jnp.maximum(running_max, score)
        new_total = running_total * jnp.exp(running_max - new_max) + jnp.exp(score - new_max)
        return (new_max, new_total)

    start_max = jnp.full((rows, assets, tile), -jnp.inf, jnp.float32)
    start_total = jnp.zeros((rows, assets, tile), jnp.float32)
    final_max, final_total = lax.fori_loop(0, levels, level_step, (start_max, start_total))
    value_tile = (0.05 * (final_max + jnp.log(final_total))).astype(jnp.bfloat16)
    return lax.all_to_all(value_tile, "skill", split_axis=0, concat_axis=2, tiled=True)


SUB = 16
STEP = 32
SCALE = math.log2(math.e) / 0.05


def split_three(mix):
    high = mix.astype(jnp.bfloat16)
    rest = mix - high.astype(jnp.float32)
    middle = rest.astype(jnp.bfloat16)
    low = (rest - middle.astype(jnp.float32)).astype(jnp.bfloat16)
    return high, middle, low


def arrange_weights(t, tiles, weights, offsets, counts, sorted_weights):
    levels, blocks, tile, _ = weights.shape

    def one_level(i, carry):
        for r in range(blocks):
            total = jnp.zeros((tile, tile), jnp.float32)
            for k in range(blocks):
                live = (offsets[k] == r) & (counts > k) & (t + r < tiles)
                total = total + jnp.where(live, weights[i, k].astype(jnp.float32), 0.0)
            total = total.astype(jnp.bfloat16)
            for q in range(tile // STEP):
                sorted_weights[q, pl.ds(pl.multiple_of(i * STEP, STEP), STEP), r * tile : (r + 1) * tile] = total[
                    q * STEP : (q + 1) * STEP
                ]
        return carry

    lax.fori_loop(0, levels, one_level, 0)


def one_chunk(window, flow, choose, sorted_weights, scaled, chosen, cont, value, levels, rows):
    for a in range(2):
        scaled[a] = flow[:, a, :] * SCALE
        chosen[a] = choose[:, a, :]
    steps = sorted_weights.shape[0]

    def multiply(q):
        cont[q % 2] = lax.dot_general(
            sorted_weights[q], window, (((1,), (1,)), ((), ())), preferred_element_type=jnp.float32
        )

    def reduce(q):
        for part in range(STEP // SUB):
            for a in range(2):
                scores = []
                for i in range(levels):
                    at = i * STEP + part * SUB
                    first = cont[q % 2, at : at + SUB, :rows]
                    second = cont[q % 2, at : at + SUB, rows:]
                    picked = jnp.where(chosen[a, i : i + 1, :] == 1, second, first)
                    scores.append(scaled[a, i : i + 1, :] + (0.96 * SCALE) * picked)
                top = scores
                while len(top) > 1:
                    top = [jnp.maximum(x, y) for x, y in zip(top[::2], top[1::2])]
                terms = [jnp.exp2(x - top[0]) for x in scores]
                while len(terms) > 1:
                    terms = [x + y for x, y in zip(terms[::2], terms[1::2])]
                start = q * STEP + part * SUB
                value[a, start : start + SUB, :] = (1.0 / SCALE) * (top[0] + jnp.log2(terms[0]))

    multiply(0)
    for q in range(steps):
        if q + 1 < steps:
            multiply(q + 1)
        reduce(q)

MESH = pl.DeviceIdType.MESH


def pick(index, table):
    chosen = table[0]
    for at, entry in enumerate(table[1:], 1):
        chosen = jnp.where(index == at, entry, chosen)
    return chosen


ARRIVE = ((1, 3, 2), (3, 2, 0), (0, 3, 1), (2, 0, 1))
WORK = ((1, 3, 2), (2, 0, 3), (0, 3, 1), (2, 0, 1))
SEND = ((2, 3, 1), (2, 3, 0), (1, 0, 3), (1, 0, 2))
PIECES = 4


def fused_kernel(
    tiles,
    offsets,
    counts,
    mix,
    values,
    weights,
    flow,
    choose,
    out,
    expected,
    window,
    sorted_weights,
    results,
    scaled,
    chosen,
    cont,
    value,
    base_send,
    base_recv,
    relay_send,
    extra_recv,
    out_send,
    out_recv,
    across_send,
    across_recv,
    over_send,
    over_recv,
    core_send,
    core_recv,
    local_sems,
):
    planes = len(SEND)
    levels, blocks, tile, _ = weights.shape
    rows = values.shape[1]
    near = tiles // planes
    reach = near + blocks - 1
    me = lax.axis_index("skill")
    y = lax.axis_index("grp")
    z = lax.div(me, 4)
    x = lax.rem(lax.div(me, 2), 2)
    core = lax.rem(me, 2)
    last = z + 1 >= planes

    def column(plane):
        return {"skill": plane * 4 + x * 2 + core}

    across = {"skill": z * 4 + (1 - x) * 2 + core}
    over = {"grp": 1 - y}
    partner = {"skill": z * 4 + x * 2 + 1 - core}

    barrier = pltpu.get_barrier_semaphore()
    for step in range(1, planes):
        pl.semaphore_signal(
            barrier, inc=1, device_id=column(lax.rem(z + step, planes)), device_id_type=MESH
        )
    for other in (across, over, partner):
        pl.semaphore_signal(barrier, inc=1, device_id=other, device_id_type=MESH)

    parts = split_three(mix[...])

    def mix_pair(pair, carry):
        for a in range(2):
            block = values[a, :, pl.ds(pl.multiple_of(pair * 2 * tile, 2 * tile), 2 * tile)]
            total = jnp.dot(parts[2], block, preferred_element_type=jnp.float32)
            total = total + jnp.dot(parts[1], block, preferred_element_type=jnp.float32)
            total = total + jnp.dot(parts[0], block, preferred_element_type=jnp.float32)
            total = total.astype(jnp.bfloat16)
            expected[pair * 2, a] = total[:, :tile]
            expected[pair * 2 + 1, a] = total[:, tile:]
        return carry

    lax.fori_loop(0, tiles // 2, mix_pair, 0)
    for r in range(blocks - 1):
        expected[tiles + r] = jnp.zeros(expected.shape[1:], jnp.bfloat16)

    def remote(source, target, send, recv, device):
        return pltpu.make_async_remote_copy(
            src_ref=source,
            dst_ref=target,
            send_sem=send,
            recv_sem=recv,
            device_id=device,
            device_id_type=MESH,
        )

    def base_copy(plane, origin, count):
        return remote(
            expected.at[pl.ds(plane * near, count)],
            window.at[origin, pl.ds(0, count)],
            base_send.at[plane],
            base_recv.at[origin],
            column(plane),
        )

    def each_base(origin, plane, act):
        wide = (plane + 1 >= origin) & (plane + 1 < planes)

        @pl.when(wide)
        def _():
            act(base_copy(plane, origin, reach))

        @pl.when(jnp.logical_not(wide))
        def _():
            act(base_copy(plane, origin, near))

    def relay_copy(origin):
        return remote(
            window.at[origin, pl.ds(0, blocks - 1)],
            window.at[origin, pl.ds(near, blocks - 1)],
            relay_send.at[origin],
            extra_recv.at[origin],
            column(lax.rem(z + planes - 1, planes)),
        )

    def out_copy(side, plane, origin):
        pair = lax.rem(x + side, 2) * 2
        return remote(
            results.at[plane, pl.ds(pair, 2)],
            out.at[pl.ds(origin * near + pair, 2)],
            out_send.at[side, plane],
            out_recv.at[side, origin],
            column(plane),
        )

    def keep_copy(side):
        pair = lax.rem(x + side, 2) * 2
        return pltpu.make_async_copy(
            results.at[z, pl.ds(pair, 2)], out.at[pl.ds(z * near + pair, 2)], local_sems.at[side]
        )

    steps = sorted_weights.shape[1]
    part = sorted_weights.shape[2] * (steps // 2) // PIECES
    per_step = sorted_weights.shape[2] // part

    def piece(which, half, index):
        return sorted_weights.at[
            which, half * (steps // 2) + index // per_step, pl.ds(index % per_step * part, part)
        ]

    mine = x * 2 + core
    foreign = (1 - x) * 2 + core

    def across_copy(which, index):
        ref = piece(which, y, index)
        return remote(ref, ref, across_send.at[index], across_recv.at[index], across)

    def over_copy(half, index):
        ref = piece(foreign, half, index)
        return remote(ref, ref, over_send.at[index], over_recv.at[index], over)

    def own_copy(which):
        ref = sorted_weights.at[which]
        return remote(ref, ref, core_send.at[2], core_recv.at[2], partner)

    def half_copy(which, half, index):
        ref = sorted_weights.at[which, pl.ds(half * (steps // 2), steps // 2)]
        return remote(ref, ref, core_send.at[index], core_recv.at[index], partner)

    pl.semaphore_wait(barrier, planes + 2)

    for step in range(planes - 1):
        each_base(z, pick(z, [order[step] for order in SEND]), lambda copy: copy.start())

    arrange_weights(
        me, tiles, weights, [offsets[0, k] for k in range(blocks)], counts[0, 0], sorted_weights.at[mine]
    )
    for index in range(PIECES):
        across_copy(mine, index).start()
    own_copy(mine).start()

    for r in range(reach):
        window[z, r] = expected[z * near + r]

    @pl.when(last)
    def _():
        for step in range(1, planes):
            for r in range(near, reach):
                window[lax.rem(z + step, planes), r] = jnp.zeros(window.shape[2:], jnp.bfloat16)

    def arrive(order):
        origin = pick(z, order)
        each_base(origin, z, lambda copy: copy.wait_recv())

        @pl.when((origin > z) & (z >= 1))
        def _():
            relay_copy(origin).start()

    def hand_on(index):
        across_copy(foreign, index).wait_recv()
        over_copy(y, index).start()

    def compute(origin, side):
        start = pl.multiple_of((origin * 4 + x * 2 + core) * rows, rows)
        flow_here = flow[:, :, pl.ds(start, rows)]
        choose_here = choose[:, :, pl.ds(start, rows)]
        first = lax.rem(x + side, 2) * 2

        def one_tile(t, inner):
            blocks_here = [window[origin, t + r].reshape(2 * rows, tile) for r in range(blocks)]
            one_chunk(
                jnp.concatenate(blocks_here, axis=1),
                flow_here,
                choose_here,
                sorted_weights.at[t],
                scaled,
                chosen,
                cont,
                value,
                levels,
                rows,
            )
            for a in range(2):
                results[origin, t, a] = value[a].T.astype(jnp.bfloat16)
            return inner

        lax.fori_loop(first, first + 2, one_tile, 0)

    own_copy(x * 2 + 1 - core).wait_recv()

    def advance(step, carry):
        side = lax.div(step, planes)
        turn = lax.rem(step + planes - 1 + side, planes)
        origin = jnp.where(turn == planes - 1, z, 0)
        for at in range(planes - 1):
            origin = jnp.where(turn == at, pick(z, [order[at] for order in WORK]), origin)

        @pl.when(step == 1)
        def _():
            arrive([order[0] for order in ARRIVE])
            hand_on(0)
            hand_on(1)
            arrive([order[1] for order in ARRIVE])

        @pl.when(step == 2)
        def _():
            hand_on(2)
            hand_on(3)
            half_copy(foreign, y, 0).start()
            arrive([order[2] for order in ARRIVE])

        @pl.when(step == 3)
        def _():
            for index in range(PIECES):
                over_copy(1 - y, index).wait_recv()
            half_copy(foreign, 1 - y, 1).start()

        @pl.when(step == planes)
        def _():
            half_copy((1 - x) * 2 + 1 - core, y, 0).wait_recv()
            half_copy((1 - x) * 2 + 1 - core, 1 - y, 1).wait_recv()

        @pl.when((side == 0) & (origin > z + 1))
        def _():
            relay_copy(origin).wait_recv()

        compute(origin, side)

        @pl.when(origin != z)
        def _():
            out_copy(side, origin, z).start()

        @pl.when(origin == z)
        def _():
            keep_copy(side).start()

        return carry

    lax.fori_loop(0, 2 * planes, advance, 0)

    for side in range(2):
        keep_copy(side).wait()
    own_copy(mine).wait_send()
    half_copy(foreign, y, 0).wait_send()
    half_copy(foreign, 1 - y, 1).wait_send()
    for index in range(PIECES):
        across_copy(mine, index).wait_send()
        over_copy(y, index).wait_send()

    def finish(step, carry):
        plane = lax.rem(z + step, planes)
        each_base(z, plane, lambda copy: copy.wait_send())

        @pl.when((plane > z) & (z >= 1))
        def _():
            relay_copy(plane).wait_send()

        for side in range(2):
            out_copy(side, plane, z).wait_send()
            out_copy(side, plane, plane).wait_recv()
        return carry

    lax.fori_loop(1, planes, finish, 0)


def on_device(value_next, income_matrix, block_weights, block_offset, block_count, asset_next, flow):
    tiles = lax.axis_size("skill")
    planes = len(SEND)
    rows, assets, skills = value_next.shape
    tile = skills // tiles
    shocks = income_matrix.shape[0]
    levels, blocks = block_weights.shape[1:3]
    mix = jnp.kron(jnp.eye(rows // shocks, dtype=jnp.float32), income_matrix)
    turned = jnp.transpose(value_next, (1, 0, 2))
    smem = pl.BlockSpec(memory_space=pltpu.SMEM)
    vmem = pl.BlockSpec(memory_space=pltpu.VMEM)
    dma = pltpu.SemaphoreType.DMA
    back = pl.pallas_call(
        functools.partial(fused_kernel, tiles),
        out_shape=jax.ShapeDtypeStruct((tiles, assets, rows, tile), jnp.bfloat16),
        in_specs=[smem, smem, vmem, vmem, vmem, vmem, vmem],
        out_specs=pl.BlockSpec(memory_space=pl.ANY),
        scratch_shapes=[
            pltpu.VMEM((tiles + blocks - 1, assets, rows, tile), jnp.bfloat16),
            pltpu.VMEM((planes, tiles // planes + blocks - 1, assets, rows, tile), jnp.bfloat16),
            pltpu.VMEM((4, tile // STEP, levels * STEP, blocks * tile), jnp.bfloat16),
            pltpu.VMEM((planes, tiles // planes, assets, rows, tile), jnp.bfloat16),
            pltpu.VMEM((assets, levels, rows), jnp.float32),
            pltpu.VMEM((assets, levels, rows), jnp.int32),
            pltpu.VMEM((2, levels * STEP, assets * rows), jnp.float32),
            pltpu.VMEM((assets, tile, rows), jnp.float32),
            dma((planes,)),
            dma((planes,)),
            dma((planes,)),
            dma((planes,)),
            dma((2, planes)),
            dma((2, planes)),
            dma((PIECES,)),
            dma((PIECES,)),
            dma((PIECES,)),
            dma((PIECES,)),
            dma((3,)),
            dma((3,)),
            dma((2,)),
        ],
        compiler_params=pltpu.CompilerParams(
            collective_id=0, has_side_effects=True, vmem_limit_bytes=48 * 1024 * 1024
        ),
    )(block_offset[0], block_count, mix, turned, block_weights[0], flow, asset_next)
    return jnp.transpose(back, (2, 1, 0, 3)).reshape(rows, assets, skills)


def solution(mesh):
    placed = (
        P("skill", "grp", None),
        P("grp", None),
        P("skill", None, None, None, None),
        P("skill", None, None),
        P("skill", None),
        P(),
        P("grp", None, None),
    )

    def body(value_next, income_matrix, *rest):
        whole = value_next.shape[0] % income_matrix.shape[0] == 0
        whole = whole and mesh.shape["skill"] == 4 * len(SEND) and mesh.shape["grp"] == 2
        return (on_device if whole else on_device_split)(value_next, income_matrix, *rest)

    return jax.shard_map(
        body, mesh=mesh, in_specs=placed, out_specs=P("skill", "grp", None), check_vma=False
    )
```

time: 95 us -> 68.1 us (0.72)
  the two profiles are of different devices: /device:TPU:16 before, /device:TPU:24 now
where the time goes in v2:
time: 68.1 us; the launch traced here: 67.8 us
  Pallas kernels  61.5 us (90%)
  local copies, waits for them, and re-layouts  5.39 us (8%)
  other arithmetic  0.82 us (1%)
    pallas_call x1, Pallas kernels, on_device(): pl.pallas_call(functools.partial(fused_kernel, tiles), out_shape=jax.Shap...  61.5 us
    reshape x1, local copies, waits for them, and re-layouts, on_device(): return jnp.transpose(back, (2, 1, 0, 3)).reshape(rows, assets, skills)  2.01 us
    unnamed x9, local copies, waits for them, and re-layouts  1.64 us

profile of v2, /device:TPU:24, one launch (start us, length us, event | category | flops | bytes accessed | tf_op | source)
XLA Modules:
  0.0 67.8 jit_solution(15941967250463110550)
XLA Ops:
  0.0 0.0 copy-start.1
  0.0 0.0 copy-start.3
  0.0 0.0 copy-start
  0.0 0.9 %copy.11.offsets = s32[16,4]{1,0:T(8,128)S(1)} copy(s32[16,4]{0,1:T(4,128)} %bitcast.11) | data formatting | bytes 512 | tf_op jit(solution)/shard_map/squeeze | solution.py:493
  0.9 0.8 %broadcast_multiply_fusion = f32[4,32,4,32]{3,2,1,0:T(4,128)S(1)} fusion(f32[32,32]{1,0:T(8,128)} %param.8, f32[4,4]{1,0:T(4,128)S(1)} %fusion), kind=kLoop, calls=%fused_computation.1 | loop fusion | flops 16384 | bytes 69696 | tf_op jit(solution)/shard_map/jit(kron)/mul | solution.py:457
  1.8 0.2 mul.27.mix
  1.9 0.0 copy-start.2
  1.9 1.6 %copy.15 = bf16[128,2,2048]{2,0,1:T(8,128)(2,1)S(1)} copy(bf16[128,2,2048]{2,1,0:T(2,128)(2,1)} %param.7) | data formatting | bytes 2097152 | tf_op args[0]
  3.6 0.0 copy-done.1
  3.6 0.0 copy-done.3
  3.6 0.0 copy-done
  3.6 0.0 copy-done.2
  3.6 61.5 %shard_map.73 = bf16[16,2,128,128]{3,2,1,0:T(8,128)(2,1)S(1)} custom-call(s32[16,4]{1,0:T(8,128)S(1)} %copy.11.offsets, s32[1,16]{1,0:T(1,128)S(1)} %copy-done.3, f32[128,128]{1,0:T(8,128)S(1)} %mul.27.mix, bf16[2,128,2048]{2,1,0:T(8,128)(2,1)S(1)} %bitcast.8, bf16[16,4,128,128]{3,2,1,0:T(8,128)(2,1)S(1)} %bitcast.9, f32[16,2,2048]{2,1,0:T(2,128)S(1)} %copy-done.1, ...), custom_call_target="tpu_custom_call" | custom-call | tf_op jit(solution)/shard_map/pallas_call | solution.py:462
  65.1 0.7 copy.12
  65.8 2.0 %copy.13 = bf16[128,2,2048]{2,1,0:T(2,128)(2,1)} copy(bf16[128,2,2048]{0,2,1:T(8,128)(2,1)S(1)} %bitcast.10) | data formatting | bytes 2097152 | tf_op jit(solution)/shard_map/reshape | solution.py:494
  (1 shorter events, 0.0 us)
Async XLA Ops:
  0.0 3.6 %copy-start.1 = (f32[16,2,2048]{2,1,0:T(2,128)S(1)}, f32[16,2,2048]{2,1,0:T(2,128)}, u32[]{:S(2)}) copy-start(f32[16,2,2048]{2,1,0:T(2,128)} %flow.1) | copy-start | bytes 786436
  0.0 3.6 %copy-start.3 = (s32[1,16]{1,0:T(1,128)S(1)}, s32[1,16]{1,0:T(1,128)}, u32[]{:S(2)}) copy-start(s32[1,16]{1,0:T(1,128)} %counts.1) | copy-start | bytes 196
  0.0 3.6 %copy-start = (bf16[1,16,4,128,128]{4,3,2,1,0:T(8,128)(2,1)S(1)}, bf16[1,16,4,128,128]{4,3,2,1,0:T(8,128)(2,1)}, u32[]{:S(2)}) copy-start(bf16[1,16,4,128,128]{4,3,2,1,0:T(8,128)(2,1)} %param.9) | copy-start | bytes 6291460
  1.9 1.7 %copy-start.2 = (s32[16,2,2048]{2,1,0:T(2,128)S(1)}, s32[16,2,2048]{2,1,0:T(2,128)}, u32[]{:S(2)}) copy-start(s32[16,2,2048]{2,1,0:T(2,128)} %choose.1) | copy-start | bytes 786436

commit v3 on v2

--- a/solution.py
+++ b/solution.py
@@ -152,15 +152,19 @@
 PIECES = 4
 
 
+def iota(shape, axis):
+    return lax.broadcasted_iota(jnp.int32, shape, axis)
+
+
 def fused_kernel(
     tiles,
-    offsets,
-    counts,
-    mix,
-    values,
-    weights,
-    flow,
-    choose,
+    offsets_in,
+    counts_in,
+    mix_in,
+    values_in,
+    weights_in,
+    flow_in,
+    choose_in,
     out,
     expected,
     window,
@@ -183,10 +187,18 @@
     core_send,
     core_recv,
     local_sems,
+    offsets,
+    counts,
+    mix,
+    values,
+    weights,
+    flow,
+    choose,
+    load_sems,
 ):
     planes = len(SEND)
     levels, blocks, tile, _ = weights.shape
-    rows = values.shape[1]
+    rows = values.shape[0]
     near = tiles // planes
     reach = near + blocks - 1
     me = lax.axis_index("skill")
@@ -203,6 +215,22 @@
     over = {"grp": 1 - y}
     partner = {"skill": z * 4 + x * 2 + 1 - core}
 
+    arrays = (
+        (values_in, values),
+        (mix_in, mix),
+        (weights_in, weights),
+        (offsets_in, offsets),
+        (counts_in, counts),
+        (flow_in, flow),
+        (choose_in, choose),
+    )
+    loads = [
+        pltpu.make_async_copy(origin, target, load_sems.at[at])
+        for at, (origin, target) in enumerate(arrays)
+    ]
+    for load in loads:
+        load.start()
+
     barrier = pltpu.get_barrier_semaphore()
     for step in range(1, planes):
         pl.semaphore_signal(
@@ -211,17 +239,32 @@
     for other in (across, over, partner):
         pl.semaphore_signal(barrier, inc=1, device_id=other, device_id_type=MESH)
 
-    parts = split_three(mix[...])
+    loads[0].wait()
+    loads[1].wait()
+    shocks = mix.shape[0]
+    both = 2 * rows
+    to_row = (iota((both, shocks), 0) % shocks == iota((both, shocks), 1)).astype(jnp.bfloat16)
+    to_column = (iota((shocks, both), 1) // 2 % shocks == iota((shocks, both), 0)).astype(jnp.bfloat16)
+    down, along = iota((both, both), 0), iota((both, both), 1)
+    same = (down // rows == along % 2) & (down % rows // shocks == along // 2 // shocks)
+
+    def spread(part):
+        wide = jnp.dot(to_row, part, preferred_element_type=jnp.float32).astype(jnp.bfloat16)
+        full = jnp.dot(wide, to_column, preferred_element_type=jnp.float32)
+        return jnp.where(same, full, 0.0).astype(jnp.bfloat16)
+
+    parts = [spread(part) for part in split_three(mix[...])]
 
     def mix_pair(pair, carry):
+        block = values[:, :, pl.ds(pl.multiple_of(pair * 2 * tile, 2 * tile), 2 * tile)]
+        block = block.reshape(both, 2 * tile)
+        total = jnp.dot(parts[2], block, preferred_element_type=jnp.float32)
+        total = total + jnp.dot(parts[1], block, preferred_element_type=jnp.float32)
+        total = total + jnp.dot(parts[0], block, preferred_element_type=jnp.float32)
+        total = total.astype(jnp.bfloat16)
         for a in range(2):
-            block = values[a, :, pl.ds(pl.multiple_of(pair * 2 * tile, 2 * tile), 2 * tile)]
-            total = jnp.dot(parts[2], block, preferred_element_type=jnp.float32)
-            total = total + jnp.dot(parts[1], block, preferred_element_type=jnp.float32)
-            total = total + jnp.dot(parts[0], block, preferred_element_type=jnp.float32)
-            total = total.astype(jnp.bfloat16)
-            expected[pair * 2, a] = total[:, :tile]
-            expected[pair * 2 + 1, a] = total[:, tile:]
+            expected[pair * 2, a] = total[a * rows : (a + 1) * rows, :tile]
+            expected[pair * 2 + 1, a] = total[a * rows : (a + 1) * rows, tile:]
         return carry
 
     lax.fori_loop(0, tiles // 2, mix_pair, 0)
@@ -267,21 +310,21 @@
             column(lax.rem(z + planes - 1, planes)),
         )
 
+    def place(side, origin):
+        column = (origin * near + lax.rem(x + side, 2) * 2) * tile
+        return out.at[:, :, pl.ds(pl.multiple_of(column, 2 * tile), 2 * tile)]
+
     def out_copy(side, plane, origin):
-        pair = lax.rem(x + side, 2) * 2
         return remote(
-            results.at[plane, pl.ds(pair, 2)],
-            out.at[pl.ds(origin * near + pair, 2)],
+            results.at[plane, side],
+            place(side, origin),
             out_send.at[side, plane],
             out_recv.at[side, origin],
             column(plane),
         )
 
     def keep_copy(side):
-        pair = lax.rem(x + side, 2) * 2
-        return pltpu.make_async_copy(
-            results.at[z, pl.ds(pair, 2)], out.at[pl.ds(z * near + pair, 2)], local_sems.at[side]
-        )
+        return pltpu.make_async_copy(results.at[z, side], place(side, z), local_sems.at[side])
 
     steps = sorted_weights.shape[1]
     part = sorted_weights.shape[2] * (steps // 2) // PIECES
@@ -316,8 +359,10 @@
     for step in range(planes - 1):
         each_base(z, pick(z, [order[step] for order in SEND]), lambda copy: copy.start())
 
+    for load in loads[2:5]:
+        load.wait()
     arrange_weights(
-        me, tiles, weights, [offsets[0, k] for k in range(blocks)], counts[0, 0], sorted_weights.at[mine]
+        me, tiles, weights, [offsets[k, 0] for k in range(blocks)], counts[0, 0], sorted_weights.at[mine]
     )
     for index in range(PIECES):
         across_copy(mine, index).start()
@@ -365,11 +410,14 @@
                 rows,
             )
             for a in range(2):
-                results[origin, t, a] = value[a].T.astype(jnp.bfloat16)
+                at = pl.ds(pl.multiple_of((t - first) * tile, tile), tile)
+                results[origin, side, a, :, at] = value[a].T.astype(jnp.bfloat16)
             return inner
 
         lax.fori_loop(first, first + 2, one_tile, 0)
 
+    for load in loads[5:]:
+        load.wait()
     own_copy(x * 2 + 1 - core).wait_recv()
 
     def advance(step, carry):
@@ -452,23 +500,19 @@
     planes = len(SEND)
     rows, assets, skills = value_next.shape
     tile = skills // tiles
-    shocks = income_matrix.shape[0]
     levels, blocks = block_weights.shape[1:3]
-    mix = jnp.kron(jnp.eye(rows // shocks, dtype=jnp.float32), income_matrix)
-    turned = jnp.transpose(value_next, (1, 0, 2))
-    smem = pl.BlockSpec(memory_space=pltpu.SMEM)
-    vmem = pl.BlockSpec(memory_space=pltpu.VMEM)
+    hbm = pl.BlockSpec(memory_space=pltpu.HBM)
     dma = pltpu.SemaphoreType.DMA
     back = pl.pallas_call(
         functools.partial(fused_kernel, tiles),
-        out_shape=jax.ShapeDtypeStruct((tiles, assets, rows, tile), jnp.bfloat16),
-        in_specs=[smem, smem, vmem, vmem, vmem, vmem, vmem],
+        out_shape=jax.ShapeDtypeStruct((assets, rows, skills), jnp.bfloat16),
+        in_specs=[hbm] * 7,
         out_specs=pl.BlockSpec(memory_space=pl.ANY),
         scratch_shapes=[
             pltpu.VMEM((tiles + blocks - 1, assets, rows, tile), jnp.bfloat16),
             pltpu.VMEM((planes, tiles // planes + blocks - 1, assets, rows, tile), jnp.bfloat16),
             pltpu.VMEM((4, tile // STEP, levels * STEP, blocks * tile), jnp.bfloat16),
-            pltpu.VMEM((planes, tiles // planes, assets, rows, tile), jnp.bfloat16),
+            pltpu.VMEM((planes, 2, assets, rows, tiles // planes // 2 * tile), jnp.bfloat16),
             pltpu.VMEM((assets, levels, rows), jnp.float32),
             pltpu.VMEM((assets, levels, rows), jnp.int32),
             pltpu.VMEM((2, levels * STEP, assets * rows), jnp.float32),
@@ -486,12 +530,20 @@
             dma((3,)),
             dma((3,)),
             dma((2,)),
+            pltpu.SMEM((blocks, levels), jnp.int32),
+            pltpu.SMEM((1, levels), jnp.int32),
+            pltpu.VMEM(income_matrix.shape, jnp.float32),
+            pltpu.VMEM(value_next.shape, jnp.bfloat16),
+            pltpu.VMEM(block_weights.shape[1:], jnp.bfloat16),
+            pltpu.VMEM(flow.shape, jnp.float32),
+            pltpu.VMEM(asset_next.shape, jnp.int32),
+            dma((7,)),
         ],
         compiler_params=pltpu.CompilerParams(
-            collective_id=0, has_side_effects=True, vmem_limit_bytes=48 * 1024 * 1024
+            collective_id=0, has_side_effects=True, vmem_limit_bytes=67043328
         ),
-    )(block_offset[0], block_count, mix, turned, block_weights[0], flow, asset_next)
-    return jnp.transpose(back, (2, 1, 0, 3)).reshape(rows, assets, skills)
+    )(block_offset[0].T, block_count, income_matrix, value_next, block_weights[0], flow, asset_next)
+    return jnp.transpose(back, (1, 0, 2))
 
 
 def solution(mesh):

time: 68.1 us -> 66.4 us (0.975)
  local copies, waits for them, and re-layouts: 5.39 us -> 3.27 us
  Pallas kernels: 61.5 us -> 62.9 us
  other arithmetic: 0.82 us -> 0 us
    transpose x1, local copies, waits for them, and re-layouts: 0.66 us -> 3.27 us  [on_device(): return jnp.transpose(back, (1, 0, 2))]
    reshape x1 -> x0, local copies, waits for them, and re-layouts: 2.01 us -> none  [on_device(): return jnp.transpose(back, (2, 1, 0, 3)).reshape(rows, assets, skills)]
    unnamed x9 -> x0, local copies, waits for them, and re-layouts: 1.64 us -> none
    pallas_call x1, Pallas kernels: 61.5 us -> 62.9 us  [on_device(): pl.pallas_call(functools.partial(fused_kernel, tiles), out_shape=jax.Shap...]
    squeeze x1 -> x0, local copies, waits for them, and re-layouts: 0.91 us -> none  [on_device(): block_offset[0]]
    mul x1 -> x0, other arithmetic: 0.82 us -> none  [on_device(): mix = jnp.kron(jnp.eye(rows // shocks, dtype=jnp.float32), income_matrix)]
where the time goes in v3:
time: 66.4 us; the launch traced here: 66.2 us
  Pallas kernels  62.9 us (95%)
  local copies, waits for them, and re-layouts  3.27 us (5%)
    pallas_call x1, Pallas kernels, on_device(): pl.pallas_call(functools.partial(fused_kernel, tiles), out_shape=jax.Shap...  62.9 us
    transpose x1, local copies, waits for them, and re-layouts, on_device(): return jnp.transpose(back, (1, 0, 2))  3.27 us

profile of v3, /device:TPU:24, one launch (start us, length us, event | category | flops | bytes accessed | tf_op | source)
XLA Modules:
  0.0 66.2 jit_solution(7012206687942875290)
XLA Ops:
  0.0 62.9 %shard_map.73 = bf16[2,128,2048]{2,1,0:T(8,128)(2,1)} custom-call(s32[4,16]{1,0:T(4,128)} %bitcast.7, s32[1,16]{1,0:T(1,128)} %counts_in.1, f32[32,32]{1,0:T(8,128)} %mix_in.1, bf16[128,2,2048]{2,1,0:T(2,128)(2,1)} %values_in.1, bf16[16,4,128,128]{3,2,1,0:T(8,128)(2,1)} %bitcast.6, f32[16,2,2048]{2,1,0:T(2,128)} %flow_in.1, s32[16,2,2048]{2,1,0:T(2,128)} %choose_in.1), custom_call_target="tpu_custom_call" | custom-call | tf_op jit(solution)/shard_map/pallas_call | solution.py:506
  62.9 3.3 %copy.8 = bf16[128,2,2048]{2,1,0:T(2,128)(2,1)} copy(bf16[128,2,2048]{2,0,1:T(8,128)(2,1)} %bitcast.5) | data formatting | bytes 2097152 | tf_op jit(solution)/shard_map/transpose | solution.py:546
